TPU v7x, 256 devices: a whole 4x4x8 slice. The times are simulated.
256 devices in a mesh: seq: 8 (over y, core), vocab: 32 (over z, x).
Axes of the slice: x: 4, y: 4, z: 8, core: 2. Of those that a mesh axis runs over, the one named last changes fastest.
Arguments:
- hidden: bfloat16 [2, 1024, 5120], P(None, 'seq'), may hold values from -128 to 128
- head_weight: bfloat16 [5120, 77824], P('seq', 'vocab'), may hold values from -1 to 1
- ref_logits: bfloat16 [2, 1024, 77824], P(None, 'seq', 'vocab'), may hold values from -320 to 320
- token_ids: int32 [2, 1024], P(None, 'seq'), may hold values from 0 to 77823
- end_pos: int32 [2], replicated, may hold values from 512 to 1023
- loss_mask: int32 [2, 1024], P(None, 'seq'), may hold values 0 or 1
- scores: float32 [2], replicated, may hold values from -8 to 8
Outputs:
- logit_grad: bfloat16 [2, 1024, 77824], P(None, 'seq', 'vocab')
- hidden_grad: bfloat16 [2, 1024, 5120], P(None, 'seq', 'vocab')
- advantages: float32 [2, 1024], P(None, 'seq')
All inputs are finite; a program needn't handle non-finite values. No bound on the sum of `loss_mask` on one device may be relied on, other than what follows from the above.
Results may differ from a plain program's by a relative error of at most 0.0039.
The roundings to bfloat16 on the way count: a program that leaves them out, or rounds other values in their place, can miss the bound.
Values may be sent and summed in bfloat16 or wider, within the bound.
No kernel may reach another device: no remote copies, remote signals or barrier semaphores. Data moves between devices by JAX's collectives and lax.ppermute only.
A program may use at most 128 MiB of HBM per device.

v0:
```python
import jax
import jax.numpy as jnp
from jax import lax
from jax.sharding import PartitionSpec as P


def from_behind(shard, axis, by):
    devices = lax.axis_size(axis)
    pairs = [(i, i + by) for i in range(devices) if 0 <= i + by < devices]
    return lax.ppermute(shard, axis, pairs)


def per_device(hidden, head_weight, ref_logits, token_ids, end_pos, loss_mask, scores):
    batch, segment, width = hidden.shape
    vocab_dev = head_weight.shape[1]
    seq_start = lax.axis_index("seq") * segment
    vocab_start = lax.axis_index("vocab") * vocab_dev
    whole_head = lax.all_gather(head_weight, "seq", axis=0, tiled=True)
    logits = jnp.dot(
        hidden.reshape(batch * segment, width), whole_head, preferred_element_type=jnp.float32
    ).reshape(batch, segment, vocab_dev)
    refs = ref_logits.astype(jnp.float32)
    local_top = jnp.max(logits, axis=2)
    local_rtop = jnp.max(refs, axis=2)
    top_policy, top_ref = lax.pmax((local_top, local_rtop), "vocab")
    expo = jnp.exp(logits - top_policy[:, :, None])
    total, ref_total, weighted = lax.psum(
        (
            jnp.sum(expo, axis=2),
            jnp.sum(jnp.exp(refs - top_ref[:, :, None]), axis=2),
            jnp.sum(expo * (logits - refs), axis=2),
        ),
        "vocab",
    )
    lse_policy = top_policy + jnp.log(total)
    lse_ref = top_ref + jnp.log(ref_total)
    kl_value = weighted / total - lse_policy + lse_ref
    position = seq_start + lax.broadcasted_iota(jnp.int32, (1, segment), 1)
    live = ((loss_mask == 1) & (position <= end_pos[:, None])).astype(jnp.float32)
    at_end = (position == end_pos[:, None]).astype(jnp.float32)
    reward = -0.01 * kl_value * live + scores[:, None] * at_end
    upper = (
        lax.broadcasted_iota(jnp.int32, (segment, segment), 0)
        >= lax.broadcasted_iota(jnp.int32, (segment, segment), 1)
    ).astype(jnp.float32)
    local_returns = jnp.dot(reward, upper, precision=lax.Precision.HIGHEST)
    totals = jnp.sum(reward, axis=1)
    carried = jnp.zeros_like(totals)
    for _ in range(lax.axis_size("seq") - 1):
        carried = from_behind(totals + carried, "seq", -1)
    returns = local_returns + carried[:, None]
    count, first_moment, second_moment = lax.psum(
        (jnp.sum(live), jnp.sum(live * returns), jnp.sum(live * returns * returns)), "seq"
    )
    count = jnp.maximum(count, 1.0)
    mean = first_moment / count
    var = second_moment / count - mean * mean
    advantages = (returns - mean) / jnp.sqrt(var + 1e-05)
    factor = live * advantages / count
    prob = jnp.exp(logits - lse_policy[:, :, None])
    column = vocab_start + lax.broadcasted_iota(jnp.int32, (1, 1, vocab_dev), 2)
    onehot = (column == token_ids[:, :, None]).astype(jnp.float32)
    logit_grad = (factor[:, :, None] * (prob - onehot)).astype(jnp.bfloat16)
    partial_grad = lax.dot_general(
        logit_grad.reshape(batch * segment, vocab_dev),
        whole_head,
        (((1,), (1,)), ((), ())),
        preferred_element_type=jnp.float32,
    ).reshape(batch, segment, width)
    hidden_grad = lax.psum_scatter(partial_grad, "vocab", scatter_dimension=2, tiled=True).astype(
        jnp.bfloat16
    )
    return (logit_grad, hidden_grad, advantages)


def solution(mesh):
    in_specs = (
        P(None, "seq", None),
        P("seq", "vocab"),
        P(None, "seq", "vocab"),
        P(None, "seq"),
        P(),
        P(None, "seq"),
        P(),
    )
    out_specs = (P(None, "seq", "vocab"), P(None, "seq", "vocab"), P(None, "seq"))
    return jax.shard_map(
        per_device, mesh=mesh, in_specs=in_specs, out_specs=out_specs, check_vma=False
    )
```

profile of v0, /device:TPU:8, one launch (start us, length us, event | category | flops | bytes accessed | tf_op | source)
XLA Modules:
  0.0 593.1 jit_solution(15525419192187923961)
XLA Ops:
  7.2 0.0 all-gather.2.cloned.1.call-start
  7.2 0.7 all-gather.2.cloned.1.call-update
  7.9 0.0 reduce-scatter.2.cloned.1.call-start
  8.0 1.5 reduce_max.24
  9.5 124.9 %all-gather.2.cloned.1.call-done = bf16[5120,2432]{1,0:T(8,128)(2,1)} async-done(((bf16[640,2432]{1,0:T(8,128)(2,1)}), bf16[5120,2432]{1,0:T(8,128)(2,1)}) %all-gather.2.cloned.1.call-update) | async-done | bytes 24903696 | tf_op jit(solution)/shard_map/all_gather | solution.py:18
  134.5 13.4 %fusion.14 = (f32[2,128]{1,0:T(2,128)S(1)}, f32[2,128,2432]{2,1,0:T(8,128)}) fusion(bf16[2,128,5120]{2,1,0:T(8,128)(2,1)S(1)} %copy-done, bf16[5120,2432]{1,0:T(8,128)(2,1)} %all-gather.2.cloned.1.call-done), kind=kOutput, calls=%fused_computation.28 | convolution fusion | flops 6375964672 | bytes 30016512 | tf_op jit(solution)/shard_map/dot_general | solution.py:19
  147.8 75.2 %all-reduce.1 = (f32[2,128]{1,0:T(2,128)S(1)}, f32[2,128]{1,0:T(2,128)S(1)}) all-reduce(f32[2,128]{1,0:T(2,128)S(1)} %get-tuple-element.23, bf16[2,128]{1,0:T(2,128)(2,1)S(1)} %reduce_max.24), channel_id=1, replica_groups=mesh['seq'=8,'vocab'=32] {'vocab'}, use_global_device_ids=true, to_apply=%region_1.0 | all-reduce | flops 512 | bytes 3584 | tf_op jit(solution)/shard_map/pmax | solution.py:25
  223.1 3.2 fusion.5
  226.3 69.6 %all-reduce = (f32[2,128]{1,0:T(2,128)S(1)}, f32[2,128]{1,0:T(2,128)S(1)}, f32[2,128]{1,0:T(2,128)S(1)}) all-reduce(f32[2,128]{1,0:T(2,128)S(1)} %get-tuple-element.4, f32[2,128]{1,0:T(2,128)S(1)} %get-tuple-element.5, f32[2,128]{1,0:T(2,128)S(1)} %get-tuple-element.3), channel_id=1, replica_groups=mesh['seq'=8,'vocab'=32] {'vocab'}, use_global_device_ids=true, to_apply=%region_5.0 | all-reduce | flops 768 | bytes 6144 | tf_op jit(solution)/shard_map/psum | solution.py:27
  296.0 0.2 fusion.12
  296.1 1.9 collective-permute-start
  298.1 1.3 collective-permute-done
  299.4 3.6 collective-permute-start.1
  302.9 1.3 collective-permute-done.1
  304.2 3.6 collective-permute-start.2
  307.8 1.3 collective-permute-done.2
  309.1 3.6 collective-permute-start.3
  312.6 1.3 collective-permute-done.3
  313.9 3.6 collective-permute-start.4
  317.5 1.3 collective-permute-done.4
  318.8 3.6 collective-permute-start.5
  322.3 1.3 collective-permute-done.5
  323.6 3.6 collective-permute-start.6
  327.2 1.3 collective-permute-done.6
  328.5 0.8 select_reduce_fusion
  329.2 12.5 %all-reduce.2 = (f32[]{:T(128)}, f32[]{:T(128)}, f32[]{:T(128)}) all-reduce(f32[]{:T(128)} %get-tuple-element.7, f32[]{:T(128)} %get-tuple-element.8, f32[]{:T(128)} %get-tuple-element.6), channel_id=1, replica_groups=mesh['seq'=8,'vocab'=32] {'seq'}, use_global_device_ids=true, to_apply=%region_16.0 | all-reduce | flops 3 | bytes 24 | tf_op jit(solution)/shard_map/psum | solution.py:52
  343.7 0.6 select_divide_fusion
  344.3 2.5 multiply_convert_fusion
  346.8 1.0 copy-done.1
  347.9 14.2 %fusion = f32[2,128,5120]{1,2,0:T(8,128)} fusion(bf16[2,128,2432]{2,1,0:T(8,128)(2,1)S(1)} %multiply_convert_fusion, bf16[5120,2432]{1,0:T(8,128)(2,1)} %all-gather.2.cloned.1.call-done), kind=kOutput, calls=%fused_computation | convolution fusion | flops 6375342080 | bytes 31391744 | tf_op jit(solution)/shard_map/dot_general | solution.py:64
  362.1 222.7 %reduce-scatter.2.cloned.1.call-done = f32[2,128,160]{1,2,0:T(8,128)} async-done(((f32[2,128,5120]{1,2,0:T(8,128)}), f32[2,128,160]{1,2,0:T(8,128)}) %reduce-scatter.2.cloned.1.call-update) | async-done | bytes 163856 | tf_op jit(solution)/shard_map/reduce_scatter | solution.py:70
  584.7 1.6 convert_element_type.21
  (20 shorter events, 0.1 us)
Async XLA Ops:
  7.2 127.3 %copy-start = (bf16[2,128,5120]{2,1,0:T(8,128)(2,1)S(1)}, bf16[2,128,5120]{2,1,0:T(8,128)(2,1)}, u32[]{:S(2)}) copy-start(bf16[2,128,5120]{2,1,0:T(8,128)(2,1)} %param.7) | copy-start | bytes 7864324
  7.2 127.3 %all-gather.2.cloned.1.call-start = ((), (), s32[]{:S(2)}) async-start(), calls=%async_computation.1 | async-start | bytes 28016640 | tf_op jit(solution)/shard_map/all_gather | solution.py:18
  7.9 576.8 %reduce-scatter.2.cloned.1.call-start = ((), (), s32[]{:S(2)}) async-start(), calls=%async_computation.2 | async-start | bytes 5406720 | tf_op jit(solution)/shard_map/reduce_scatter | solution.py:70
  147.8 148.1 %copy-start.3 = (s32[2,128]{1,0:T(2,128)S(1)}, s32[2,128]{1,0:T(2,128)}, u32[]{:S(2)}) copy-start(s32[2,128]{1,0:T(2,128)} %param.12) | copy-start | bytes 3076
  147.8 148.1 %copy-start.4 = (f32[2]{0:T(128)S(1)}, f32[2]{0:T(128)}, u32[]{:S(2)}) copy-start(f32[2]{0:T(128)} %param.13) | copy-start | bytes 28
  147.8 148.1 %copy-start.5 = (s32[2]{0:T(128)S(1)}, s32[2]{0:T(128)}, u32[]{:S(2)}) copy-start(s32[2]{0:T(128)} %param.11) | copy-start | bytes 28
  147.8 196.5 %copy-start.2 = (s32[2,128]{1,0:T(2,128)S(1)}, s32[2,128]{1,0:T(2,128)}, u32[]{:S(2)}) copy-start(s32[2,128]{1,0:T(2,128)} %param.10) | copy-start | bytes 3076
  296.1 3.2 collective-permute-start
  299.4 4.8 collective-permute-start.1
  304.2 4.8 collective-permute-start.2
  309.1 4.8 collective-permute-start.3
  313.9 4.8 collective-permute-start.4
  318.8 4.8 collective-permute-start.5
  323.6 4.8 collective-permute-start.6
  346.8 1.0 copy-start.1
Sparse Core Ops, SparseCore 0:
  9.8 124.5 all-gather.1
  362.2 222.4 reduce-scatter.1
where the time goes:
time: 594 us; the launch traced here: 593 us
  waiting for transfers between devices  357 us (60%)
  blocking collectives  157 us (26%)
  matrix products  28.3 us (5%)
  starting transfers between devices  23.4 us (4%)
  between operations  16.2 us (3%)
  other arithmetic  9.68 us (2%)
    reduce_scatter x1, waiting for transfers between devices, per_device(): lax.psum_scatter(partial_grad, 'vocab', scatter_dimension=2, tiled=True)  223 us
    all_gather x1, waiting for transfers between devices, per_device(): whole_head = lax.all_gather(head_weight, 'seq', axis=0, tiled=True)  125 us
    pmax x1, blocking collectives, per_device(): top_policy, top_ref = lax.pmax((local_top, local_rtop), 'vocab')  75.2 us
    psum x1, blocking collectives, per_device(): lax.psum((jnp.sum(expo, axis=2), jnp.sum(jnp.exp(refs - top_ref[:, :, Non...  69.6 us
    ppermute x7, starting transfers between devices, from_behind(): return lax.ppermute(shard, axis, pairs)  23.3 us
    dot_general x1, matrix products, per_device(): lax.dot_general(logit_grad.reshape(batch * segment, vocab_dev), whole_hea...  14.2 us
    dot_general x1, matrix products, per_device(): jnp.dot(hidden.reshape(batch * segment, width), whole_head, preferred_ele...  13.4 us
    psum x1, blocking collectives, per_device(): lax.psum((jnp.sum(live), jnp.sum(live * returns), jnp.sum(live * returns...  12.5 us
  transfers between devices with their start and end apart: 9, of which 9 were waited for; matrix products, arithmetic and copies ran while one was open for 0% of the time, Pallas kernels for 0%

commit v1 on v0

--- a/solution.py
+++ b/solution.py
@@ -2,6 +2,7 @@
 import jax.numpy as jnp
 from jax import lax
 from jax.sharding import PartitionSpec as P
+from jax.lax import all_to_all, axis_size
 
 
 def from_behind(shard, axis, by):
@@ -15,7 +16,16 @@
     vocab_dev = head_weight.shape[1]
     seq_start = lax.axis_index("seq") * segment
     vocab_start = lax.axis_index("vocab") * vocab_dev
-    whole_head = lax.all_gather(head_weight, "seq", axis=0, tiled=True)
+
+    def fix_leaf(a0):
+        fields = []
+        axis_n = axis_size("seq")
+        for jj in range(a0.ndim):
+            fields.append(axis_n if jj == 0 else 1)
+        raw_out = jnp.tile(a0, fields)
+        return all_to_all(raw_out, "seq", split_axis=0, concat_axis=0, tiled=True)
+
+    whole_head = fix_leaf(head_weight)
     logits = jnp.dot(
         hidden.reshape(batch * segment, width), whole_head, preferred_element_type=jnp.float32
     ).reshape(batch, segment, vocab_dev)

time: 594 us -> 760 us (1.28)
  waiting for transfers between devices: 357 us -> 499 us
  local copies, waits for them, and re-layouts: 1.05 us -> 15.8 us
  starting transfers between devices: 23.4 us -> 31.8 us
    all_to_all x0 -> x1, waiting for transfers between devices: none -> 269 us  [fix_leaf(): return all_to_all(raw_out, 'seq', split_axis=0, concat_axis=0, tiled=True)]
    all_gather x1 -> x0, waiting for transfers between devices: 125 us -> none  [per_device(): whole_head = lax.all_gather(head_weight, 'seq', axis=0, tiled=True)]
    another operation x0 -> x1, local copies, waits for them, and re-layouts: none -> 14.7 us  [fix_leaf(): raw_out = jnp.tile(a0, fields)]
    all_to_all x0 -> x1, starting transfers between devices: none -> 8.49 us  [fix_leaf(): return all_to_all(raw_out, 'seq', split_axis=0, concat_axis=0, tiled=True)]
where the time goes in v1:
time: 760 us; the launch traced here: 759 us
  waiting for transfers between devices  499 us (66%)
  blocking collectives  158 us (21%)
  starting transfers between devices  31.8 us (4%)
  matrix products  28.3 us (4%)
  between operations  16.1 us (2%)
  local copies, waits for them, and re-layouts  15.8 us (2%)
  other arithmetic  9.68 us (1%)
    all_to_all x1, waiting for transfers between devices, fix_leaf(): return all_to_all(raw_out, 'seq', split_axis=0, concat_axis=0, tiled=True)  269 us
    reduce_scatter x1, waiting for transfers between devices, per_device(): lax.psum_scatter(partial_grad, 'vocab', scatter_dimension=2, tiled=True)  221 us
    pmax x1, blocking collectives, per_device(): top_policy, top_ref = lax.pmax((local_top, local_rtop), 'vocab')  76.1 us
    psum x1, blocking collectives, per_device(): lax.psum((jnp.sum(expo, axis=2), jnp.sum(jnp.exp(refs - top_ref[:, :, Non...  69.6 us
    ppermute x7, starting transfers between devices, from_behind(): return lax.ppermute(shard, axis, pairs)  23.3 us
  transfers between devices with their start and end apart: 9, of which 9 were waited for; matrix products, arithmetic and copies ran while one was open for 0% of the time, Pallas kernels for 0%

profile of v1, /device:TPU:8, one launch (start us, length us, event | category | flops | bytes accessed | tf_op | source)
XLA Modules:
  0.0 758.7 jit_solution(6258219236786466544)
XLA Ops:
  7.2 14.7 %tile.2 = bf16[8,640,2432]{2,1,0:T(8,128)(2,1)} broadcast(bf16[640,2432]{1,0:T(8,128)(2,1)} %param.8), dimensions={1,2} | broadcast | bytes 28016640 | tf_op jit(solution)/shard_map/tile | solution.py:25
  21.9 8.5 %all-to-all-start = ((bf16[8,640,2432]{2,1,0:T(8,128)(2,1)}), bf16[8,640,2432]{2,1,0:T(8,128)(2,1)}, u32[]{:S(2)}, u32[]{:S(2)}) async-start(bf16[8,640,2432]{2,1,0:T(8,128)(2,1)} %tile.2), calls=%async_computation | async-start | bytes 49807360 | tf_op jit(solution)/shard_map/all_to_all | solution.py:26
  30.4 1.5 reduce_max.24
  31.9 268.7 %all-to-all-done = bf16[8,640,2432]{2,1,0:T(8,128)(2,1)} async-done(((bf16[8,640,2432]{2,1,0:T(8,128)(2,1)}), bf16[8,640,2432]{2,1,0:T(8,128)(2,1)}, u32[]{:S(2)}, u32[]{:S(2)}) %all-to-all-start) | async-done | bytes 24903712 | tf_op jit(solution)/shard_map/all_to_all | solution.py:26
  300.6 13.4 %fusion.10 = (f32[2,128]{1,0:T(2,128)S(1)}, f32[2,128,2432]{2,1,0:T(8,128)}) fusion(bf16[2,128,5120]{2,1,0:T(8,128)(2,1)S(1)} %copy-done, bf16[5120,2432,1]{1,0,2:T(8,128)(2,1)} %bitcast.1), kind=kOutput, calls=%fused_computation.24 | convolution fusion | flops 6375964672 | bytes 30016512 | tf_op jit(solution)/shard_map/dot_general | solution.py:29
  314.0 76.1 %all-reduce.1 = (f32[2,128]{1,0:T(2,128)S(1)}, f32[2,128]{1,0:T(2,128)S(1)}) all-reduce(f32[2,128]{1,0:T(2,128)S(1)} %get-tuple-element.23, bf16[2,128]{1,0:T(2,128)(2,1)S(1)} %reduce_max.24), channel_id=1, replica_groups=mesh['seq'=8,'vocab'=32] {'vocab'}, use_global_device_ids=true, to_apply=%region_1.0 | all-reduce | flops 512 | bytes 3584 | tf_op jit(solution)/shard_map/pmax | solution.py:35
  390.1 3.2 fusion.1
  393.3 69.6 %all-reduce = (f32[2,128]{1,0:T(2,128)S(1)}, f32[2,128]{1,0:T(2,128)S(1)}, f32[2,128]{1,0:T(2,128)S(1)}) all-reduce(f32[2,128]{1,0:T(2,128)S(1)} %get-tuple-element.4, f32[2,128]{1,0:T(2,128)S(1)} %get-tuple-element.5, f32[2,128]{1,0:T(2,128)S(1)} %get-tuple-element.3), channel_id=1, replica_groups=mesh['seq'=8,'vocab'=32] {'vocab'}, use_global_device_ids=true, to_apply=%region_5.0 | all-reduce | flops 768 | bytes 6144 | tf_op jit(solution)/shard_map/psum | solution.py:37
  463.0 0.2 fusion.8
  463.2 1.9 collective-permute-start
  465.1 1.3 collective-permute-done
  466.4 3.6 collective-permute-start.1
  469.9 1.3 collective-permute-done.1
  471.2 3.6 collective-permute-start.2
  474.8 1.3 collective-permute-done.2
  476.1 3.6 collective-permute-start.3
  479.6 1.3 collective-permute-done.3
  480.9 3.6 collective-permute-start.4
  484.5 1.3 collective-permute-done.4
  485.8 3.6 collective-permute-start.5
  489.3 1.3 collective-permute-done.5
  490.6 3.6 collective-permute-start.6
  494.2 1.3 collective-permute-done.6
  495.5 0.8 select_reduce_fusion
  496.2 12.5 %all-reduce.2 = (f32[]{:T(128)}, f32[]{:T(128)}, f32[]{:T(128)}) all-reduce(f32[]{:T(128)} %get-tuple-element.7, f32[]{:T(128)} %get-tuple-element.8, f32[]{:T(128)} %get-tuple-element.6), channel_id=1, replica_groups=mesh['seq'=8,'vocab'=32] {'seq'}, use_global_device_ids=true, to_apply=%region_16.0 | all-reduce | flops 3 | bytes 24 | tf_op jit(solution)/shard_map/psum | solution.py:62
  510.7 0.6 select_divide_fusion
  511.4 2.5 multiply_convert_fusion
  513.9 1.0 copy-done.1
  514.9 14.2 %fusion.11 = f32[2,128,5120]{1,2,0:T(8,128)} fusion(bf16[2,128,2432]{2,1,0:T(8,128)(2,1)S(1)} %multiply_convert_fusion, bf16[5120,2432,1]{1,0,2:T(8,128)(2,1)} %bitcast.1), kind=kOutput, calls=%fused_computation.25 | convolution fusion | flops 6375342080 | bytes 31391744 | tf_op jit(solution)/shard_map/dot_general | solution.py:74
  529.1 0.0 reduce-scatter.2.cloned.1.call-update
  529.1 221.2 %reduce-scatter.2.cloned.1.call-done = f32[2,128,160]{1,2,0:T(8,128)} async-done(((f32[2,128,5120]{1,2,0:T(8,128)}), f32[2,128,160]{1,2,0:T(8,128)}) %reduce-scatter.2.cloned.1.call-update) | async-done | bytes 163856 | tf_op jit(solution)/shard_map/reduce_scatter | solution.py:80
  750.3 1.6 convert_element_type.21
  (20 shorter events, 0.1 us)
Async XLA Ops:
  7.2 293.5 %copy-start = (bf16[2,128,5120]{2,1,0:T(8,128)(2,1)S(1)}, bf16[2,128,5120]{2,1,0:T(8,128)(2,1)}, u32[]{:S(2)}) copy-start(bf16[2,128,5120]{2,1,0:T(8,128)(2,1)} %param.7) | copy-start | bytes 7864324
  21.9 278.7 %all-to-all-start = ((bf16[8,640,2432]{2,1,0:T(8,128)(2,1)}), bf16[8,640,2432]{2,1,0:T(8,128)(2,1)}, u32[]{:S(2)}, u32[]{:S(2)}) async-start(bf16[8,640,2432]{2,1,0:T(8,128)(2,1)} %tile.2), calls=%async_computation | async-start | bytes 49807360 | tf_op jit(solution)/shard_map/all_to_all | solution.py:26
  30.4 719.9 %reduce-scatter.2.cloned.1.call-start = ((), (), s32[]{:S(2)}) async-start(), calls=%async_computation.2 | async-start | bytes 5406720 | tf_op jit(solution)/shard_map/reduce_scatter | solution.py:80
  314.0 149.0 %copy-start.3 = (s32[2,128]{1,0:T(2,128)S(1)}, s32[2,128]{1,0:T(2,128)}, u32[]{:S(2)}) copy-start(s32[2,128]{1,0:T(2,128)} %param.12) | copy-start | bytes 3076
  314.0 149.0 %copy-start.4 = (f32[2]{0:T(128)S(1)}, f32[2]{0:T(128)}, u32[]{:S(2)}) copy-start(f32[2]{0:T(128)} %param.13) | copy-start | bytes 28
  314.0 149.0 %copy-start.5 = (s32[2]{0:T(128)S(1)}, s32[2]{0:T(128)}, u32[]{:S(2)}) copy-start(s32[2]{0:T(128)} %param.11) | copy-start | bytes 28
  314.0 197.4 %copy-start.2 = (s32[2,128]{1,0:T(2,128)S(1)}, s32[2,128]{1,0:T(2,128)}, u32[]{:S(2)}) copy-start(s32[2,128]{1,0:T(2,128)} %param.10) | copy-start | bytes 3076
  463.2 3.2 collective-permute-start
  466.4 4.8 collective-permute-start.1
  471.2 4.8 collective-permute-start.2
  476.1 4.8 collective-permute-start.3
  480.9 4.8 collective-permute-start.4
  485.8 4.8 collective-permute-start.5
  490.6 4.8 collective-permute-start.6
  513.9 1.0 copy-start.1
Sparse Core Ops, SparseCore 0:
  529.2 221.0 reduce-scatter.1
